TPU v7x, 32 devices: a whole 2x2x4 slice. The times are simulated.
32 devices in a mesh: section: 4 (over y, core), expert: 8 (over z, x).
Axes of the slice: x: 2, y: 2, z: 4, core: 2. Of those that a mesh axis runs over, the one named last changes fastest.
Arguments:
- acts: bfloat16 [4, 512, 2048], P('section', 'expert'), may hold values from -6 to 6
- norm_gains: float32 [4, 2, 2048], P('section'), may hold values from 0.5 to 5.5
- w_query: bfloat16 [4, 2048, 1024], P('section', None, 'expert'), may hold values from -0.125 to 0.125
- w_keyval: bfloat16 [4, 2048, 4, 256], P('section', 'expert'), may hold values from -0.125 to 0.125
- w_out: bfloat16 [4, 1024, 2048], P('section', 'expert'), may hold values from -0.5 to 0.5
- w_gate_up: bfloat16 [4, 32, 2048, 1536], P('section', 'expert'), may hold values from -0.125 to 0.125
- w_down: bfloat16 [4, 32, 768, 2048], P('section', 'expert'), may hold values from -0.21875 to 0.21875
- expert_ids: int32 [4, 512, 8], P('section', 'expert'), may hold values from 0 to 31, all different within a row; in each aligned block of 64 rows (0 to 63, 64 to 127, ..., all dimensions but the last counted through in order) at most 24 rows name the same one
- gate_weights: float32 [4, 512, 8], P('section', 'expert'), may hold values from 0.05 to 0.3
- segment_ids: int32 [4, 512], P('section'), may hold values from 0 to 15, never falling along the last dimension, each value on 1 to 128 neighbouring positions
Outputs:
- handed: bfloat16 [4, 512, 2048], P('section', 'expert')
Inputs may be any that keep to these rules, and one draw needn't show every extreme that they name: `expert_ids`: A token names 8 different experts. In each section the tokens of one index of expert (aligned blocks of 64 tokens) name no expert more than 24 times, a bound that some block reaches. `segment_ids`: never falling along a section's positions; a segment holds at most 128 positions, and one exactly that many.
All inputs are finite; a program needn't handle non-finite values.
Results may differ from a plain program's by a relative error of at most 0.015.
The roundings to bfloat16 on the way count: a program that leaves them out, or rounds other values in their place, can miss the bound.
Values may be sent and summed in bfloat16 or wider, within the bound.
A program may use at most 128 MiB of HBM per device.

v0:
```python
import math
import jax
import jax.numpy as jnp
from jax import lax
from jax.sharding import PartitionSpec as P

HD = 128
KV = 4
EXPERTS = 32
TOPK = 8
CAP = 24
EPS = 1e-06
ROPE_BASE = 1000000.0


def shifted_2(x, axis, by):
    length = lax.axis_size(axis)
    return lax.ppermute(x, axis, [(i, (i + by) % length) for i in range(length)])


def rms_scale(values, gain_row):
    mean_sq = jnp.mean(values * values, axis=-1, keepdims=True)
    return values * lax.rsqrt(mean_sq + EPS) * gain_row


def rotate(values, positions):
    half_width = values.shape[-1] // 2
    frequency = ROPE_BASE ** (-jnp.arange(half_width, dtype=jnp.float32) * 2.0 / values.shape[-1])
    angles = positions[:, None] * frequency[None, :]
    cosines = jnp.cos(angles)[:, None, :]
    sine_table = jnp.sin(angles)[:, None, :]
    leading = values[..., :half_width]
    trailing = values[..., half_width:]
    return jnp.concatenate(
        [leading * cosines - trailing * sine_table, trailing * cosines + leading * sine_table],
        axis=-1,
    )


def head_block(q_block, key_rows, value_rows, seg_block, seg_all, pos_block, pos_all, score_scale):
    scores = (
        jnp.einsum("qhd,kd->hqk", q_block, key_rows, preferred_element_type=jnp.float32)
        * score_scale
    )
    allowed = (seg_block[:, None] == seg_all[None, :]) & (pos_all[None, :] <= pos_block[:, None])
    scores = jnp.where(allowed[None], scores, -1e30)
    row_max = jnp.max(scores, axis=-1, keepdims=True)
    shifted = jnp.exp(scores - row_max)
    probability = (shifted / jnp.sum(shifted, axis=-1, keepdims=True)).astype(jnp.bfloat16)
    return jnp.einsum(
        "hqk,kd->qhd", probability, value_rows, preferred_element_type=jnp.float32
    ).astype(jnp.bfloat16)


def expert_rows(grouped, gate_up, down_proj):
    gate_up_out = jnp.einsum("necd,edf->necf", grouped, gate_up, preferred_element_type=jnp.float32)
    half_width = down_proj.shape[1]
    hidden = (jax.nn.silu(gate_up_out[..., :half_width]) * gate_up_out[..., half_width:]).astype(
        jnp.bfloat16
    )
    return jnp.einsum(
        "necf,efd->necd", hidden, down_proj, preferred_element_type=jnp.float32
    ).astype(jnp.bfloat16)


def send_back(results):
    return lax.all_to_all(results, "expert", split_axis=0, concat_axis=0, tiled=True)


def per_device(
    acts,
    norm_gains,
    w_query,
    w_keyval,
    w_out,
    w_gate_up,
    w_down,
    expert_ids,
    gate_weights,
    segment_ids,
):
    device_count = lax.axis_size("expert")
    my_index = lax.axis_index("expert")
    tok_rows = acts.shape[1]
    width = acts.shape[2]
    head_dev = w_query.shape[2] // HD
    local_experts = w_gate_up.shape[1]
    heads_total = head_dev * device_count
    gains = norm_gains[0]
    x_wide = acts[0].astype(jnp.float32)
    normed = rms_scale(x_wide, gains[0]).astype(jnp.bfloat16)
    kv_index = my_index * head_dev // (heads_total // KV)
    query_weight = w_query[0]
    gathered_keyval = lax.all_gather(w_keyval[0], "expert", axis=0, tiled=True)
    head_keyval = lax.dynamic_index_in_dim(gathered_keyval, kv_index, 1, keepdims=False)
    row_piece = lax.all_gather(normed, "expert", axis=0, tiled=True)
    piece_rows = row_piece.shape[0]
    positions = jnp.arange(piece_rows).astype(jnp.float32)
    query_piece_rows = row_piece.shape[0]
    query_positions = jnp.arange(query_piece_rows).astype(jnp.float32)
    queries = jnp.dot(row_piece, query_weight, preferred_element_type=jnp.float32).reshape(
        query_piece_rows, head_dev, HD
    )
    queries = (
        rotate(queries, query_positions)
        .astype(jnp.bfloat16)
        .reshape(query_piece_rows, head_dev * HD)
    )
    keyval = jnp.dot(row_piece, head_keyval, preferred_element_type=jnp.float32)
    key_rows = rotate(keyval[:, None, :HD], positions).astype(jnp.bfloat16).reshape(piece_rows, HD)
    value_rows = keyval[:, HD:].astype(jnp.bfloat16)
    projected = jnp.concatenate([queries, key_rows, value_rows], axis=1)
    tokens = projected.shape[0]
    all_queries = projected[:, : head_dev * HD].reshape(tokens, head_dev, HD)
    all_keys = projected[:, head_dev * HD : (head_dev + 1) * HD]
    all_values = projected[:, (head_dev + 1) * HD :]
    segments = segment_ids[0]
    all_positions = jnp.arange(tokens)
    q_rows = min(512, tokens)
    score_scale = 1.0 / math.sqrt(HD)

    def attend(first_row):
        q_block = lax.dynamic_slice_in_dim(all_queries, first_row, q_rows, 0)
        seg_block = lax.dynamic_slice_in_dim(segments, first_row, q_rows, 0)
        pos_block = first_row + jnp.arange(q_rows)
        return head_block(
            q_block,
            all_keys,
            all_values,
            seg_block,
            segments,
            pos_block,
            all_positions,
            score_scale,
        )

    block_starts = jnp.arange(tokens // q_rows) * q_rows
    attended = lax.map(attend, block_starts).reshape(tokens, head_dev * HD)
    out_weight = w_out[0]
    attention = lax.psum_scatter(
        jnp.dot(attended, out_weight, preferred_element_type=jnp.float32).astype(jnp.bfloat16),
        "expert",
        scatter_dimension=0,
        tiled=True,
    ).astype(jnp.float32)
    middle_wide = (x_wide + attention).astype(jnp.bfloat16).astype(jnp.float32)
    mixer_in = rms_scale(middle_wide, gains[1]).astype(jnp.bfloat16)
    routes_flat = expert_ids[0].reshape(-1)
    onehot = (routes_flat[:, None] == jnp.arange(EXPERTS, dtype=jnp.int32)[None, :]).astype(
        jnp.int32
    )
    earlier = jnp.cumsum(onehot, axis=0) - onehot
    slot_rank = jnp.sum(earlier * onehot, axis=1)
    slot_index = routes_flat * CAP + slot_rank
    routed = jnp.repeat(mixer_in, TOPK, axis=0)
    send_rows = (
        jnp.zeros((EXPERTS * CAP, width), jnp.bfloat16)
        .at[slot_index]
        .set(routed)
        .reshape(EXPERTS, CAP, width)
    )
    gate_up = w_gate_up[0]
    down_proj = w_down[0]
    received = lax.all_to_all(send_rows, "expert", split_axis=0, concat_axis=0, tiled=True)
    source_count = received.shape[0] // local_experts
    grouped = received.reshape(source_count, local_experts, received.shape[1], width)
    outputs = expert_rows(grouped, gate_up, down_proj)
    returned = send_back(outputs.reshape(received.shape))
    picked = (
        returned.reshape(EXPERTS * CAP, width)[slot_index]
        .astype(jnp.float32)
        .reshape(tok_rows, TOPK, width)
    )
    mixed = jnp.sum(picked * gate_weights[0][:, :, None], axis=1)
    result = (middle_wide + mixed).astype(jnp.bfloat16)
    handed = shifted_2(result, "section", 1)
    return handed[None]


def solution(mesh):
    placed = (
        P("section", "expert", None),
        P("section", None, None),
        P("section", None, "expert"),
        P("section", "expert", None, None),
        P("section", "expert", None),
        P("section", "expert", None, None),
        P("section", "expert", None, None),
        P("section", "expert", None),
        P("section", "expert", None),
        P("section", None),
    )
    return jax.shard_map(
        per_device,
        mesh=mesh,
        in_specs=placed,
        out_specs=P("section", "expert", None),
        check_vma=False,
    )
```

profile of v0, /device:TPU:0, one launch (start us, length us, event | category | flops | bytes accessed | tf_op | source)
XLA Modules:
  0.0 406.4 jit_solution(9805289773962117961)
XLA Ops:
  6.5 0.8 fusion.77
  7.4 1.1 fusion.34
  8.5 1.8 fusion.36
  10.3 1.9 copy.12
  12.4 50.0 %all-gather.4.cloned.1.call-done = bf16[512,2048]{1,0:T(8,128)(2,1)} async-done(((bf16[64,2048]{1,0:T(8,128)(2,1)}), bf16[512,2048]{1,0:T(8,128)(2,1)}) %all-gather.4.cloned.1.call-update) | async-done | bytes 2097168 | tf_op jit(solution)/shard_map/all_gather | solution.py:96
  62.4 2.5 convolution_bitcast_fusion
  64.9 71.6 %all-gather.6.cloned.1.call-done = bf16[1,2048,4,256]{3,1,2,0:T(8,128)(2,1)} async-done(((bf16[1,256,4,256]{3,1,2,0:T(8,128)(2,1)}), bf16[1,2048,4,256]{3,1,2,0:T(8,128)(2,1)}) %all-gather.6.cloned.1.call-update) | async-done | bytes 4194320 | tf_op jit(solution)/shard_map/all_gather | solution.py:94
  136.5 2.6 fusion.24
  139.1 0.6 fusion.70
  139.8 0.4 fusion.78
  140.1 0.2 fusion.29
  140.4 2.4 convolution_convert_fusion
  142.8 0.1 eq.59
  143.0 1.2 reduce-window.6
  144.2 0.2 slice_reduce_fusion
  144.6 0.1 mul.210
  144.7 0.1 fusion.68
  144.8 64.6 %reduce-scatter.2.cloned.1.call-done = bf16[64,2048]{1,0:T(8,128)(2,1)} async-done(((bf16[512,2048]{1,0:T(8,128)(2,1)}), bf16[64,2048]{1,0:T(8,128)(2,1)}) %reduce-scatter.2.cloned.1.call-update) | async-done | bytes 262160 | tf_op jit(solution)/shard_map/reduce_scatter | solution.py:140
  209.4 1.1 fusion.30
  210.6 1.8 fusion.32
  212.3 5.0 %scatter_custom_fusion = bf16[768,2048]{1,0:T(8,128)(2,1)S(1)} fusion(s32[512]{0:T(512)S(1)} %bitcast.115, bf16[]{:T(256)} %constant.73.clone.1, bf16[64,2048]{1,0:T(8,128)(2,1)} %fusion.32), kind=kCustom, calls=%fused_computation.15 | custom fusion | bytes 3407874 | tf_op jit(solution)/shard_map/scatter | solution.py:159
  217.3 72.9 %all_to_all.10 = bf16[32,24,2048]{2,1,0:T(8,128)(2,1)S(1)} all-to-all(bf16[32,24,2048]{2,1,0:T(8,128)(2,1)S(1)} %bitcast.110), channel_id=1, replica_groups=mesh['section'=4,'expert'=8] {'expert'}, dimensions={0} | all-to-all | bytes 6291456 | tf_op jit(solution)/shard_map/all_to_all | solution.py:164
  290.3 10.8 %fusion.5 = f32[8,4,24,1536]{3,2,0,1:T(8,128)S(1)} fusion(bf16[1,4,2048,1536]{3,2,1,0:T(8,128)(2,1)} %param.15, bf16[8,4,24,2048]{3,2,1,0:T(8,128)(2,1)S(1)} %bitcast.111), kind=kOutput, calls=%fused_computation.8 | convolution fusion | flops 4831838208 | bytes 33030144 | tf_op jit(solution)/shard_map/necd,edf->necf/dot_general | solution.py:56
  301.1 7.3 %fusion.12 = bf16[8,4,24,2048]{3,2,0,1:T(8,128)(2,1)S(1)} fusion(bf16[1,4,768,2048]{3,2,1,0:T(8,128)(2,1)} %param.16, f32[8,4,24,1536]{3,2,0,1:T(8,128)S(1)} %fusion.5), kind=kOutput, calls=%fused_computation.11 | convolution fusion | flops 2421030912 | bytes 20447232 | tf_op jit(solution)/shard_map/necf,efd->necd/dot_general | solution.py:61
  308.4 1.9 copy.18
  310.3 4.6 %all-to-all-start.1 = ((bf16[32,24,2048]{2,1,0:T(8,128)(2,1)}), bf16[32,24,2048]{2,1,0:T(8,128)(2,1)}, u32[]{:S(2)}, u32[]{:S(2)}) async-start(bf16[32,24,2048]{2,1,0:T(8,128)(2,1)} %bitcast.34), calls=%async_computation.2 | async-start | bytes 6291456 | tf_op jit(solution)/shard_map/all_to_all | solution.py:67
  315.0 69.5 %all-to-all-done.1 = bf16[32,24,2048]{2,1,0:T(8,128)(2,1)} async-done(((bf16[32,24,2048]{2,1,0:T(8,128)(2,1)}), bf16[32,24,2048]{2,1,0:T(8,128)(2,1)}, u32[]{:S(2)}, u32[]{:S(2)}) %all-to-all-start.1) | async-done | bytes 3145760 | tf_op jit(solution)/shard_map/all_to_all | solution.py:67
  384.5 6.8 %gather_fusion = bf16[512,2048]{1,0:T(8,128)(2,1)S(1)} fusion(bf16[768,2048]{1,0:T(8,128)(2,1)} %bitcast.35, s32[1024]{0:T(1024)S(1)} %pad_clamp_fusion), kind=kCustom, calls=%fused_computation | custom fusion | bytes 4196352 | tf_op jit(solution)/shard_map/gather | solution.py:170
  391.3 1.8 fusion.4
  393.2 0.1 fusion.33
  393.3 5.8 %collective-permute-done = bf16[64,2048]{1,0:T(8,128)(2,1)S(1)} collective-permute-done((bf16[64,2048]{1,0:T(8,128)(2,1)S(1)}, bf16[64,2048]{1,0:T(8,128)(2,1)S(1)}, u32[]{:S(2)}, u32[]{:S(2)}) %collective-permute-start) | collective-permute-done | bytes 262176 | tf_op jit(solution)/shard_map/ppermute | solution.py:18
  399.1 0.7 copy.27
  (36 shorter events, 0.7 us)
Async XLA Ops:
  6.5 133.8 %copy-start = (bf16[1,128,2048]{2,1,0:T(8,128)(2,1)S(1)}, bf16[1,128,2048]{2,1,0:T(8,128)(2,1)}, u32[]{:S(2)}) copy-start(bf16[1,128,2048]{2,1,0:T(8,128)(2,1)} %param.14) | copy-start | bytes 1572868
  6.5 55.9 %all-gather.4.cloned.1.call-start = ((), (), s32[]{:S(2)}) async-start(), calls=%async_computation.3 | async-start | bytes 2359296 | tf_op jit(solution)/shard_map/all_gather | solution.py:96
  10.3 126.2 %all-gather.6.cloned.1.call-start = ((), (), s32[]{:S(2)}) async-start(), calls=%async_computation.5 | async-start | bytes 4718592 | tf_op jit(solution)/shard_map/all_gather | solution.py:94
  12.3 197.1 %reduce-scatter.2.cloned.1.call-start = ((), (), s32[]{:S(2)}) async-start(), calls=%async_computation.4 | async-start | bytes 2359296 | tf_op jit(solution)/shard_map/reduce_scatter | solution.py:140
  64.9 74.8 %copy-start.6 = (s32[1,512]{1,0:T(1,128)S(1)}, s32[1,512]{1,0:T(1,128)}, u32[]{:S(2)}) copy-start(s32[1,512]{1,0:T(1,128)} %param.19) | copy-start | bytes 6148
  140.3 2.4 copy-start.4
  140.4 69.0 %copy-start.2 = (bf16[1,64,2048]{2,1,0:T(8,128)(2,1)S(1)}, bf16[1,64,2048]{2,1,0:T(8,128)(2,1)}, u32[]{:S(2)}) copy-start(bf16[1,64,2048]{2,1,0:T(8,128)(2,1)} %param.10) | copy-start | bytes 786436
  310.3 4.6 %copy-start.5 = (f32[1,64,8]{1,2,0:T(8,128)S(1)}, f32[1,64,8]{1,2,0:T(8,128)}, u32[]{:S(2)}) copy-start(f32[1,64,8]{1,2,0:T(8,128)} %param.18) | copy-start | bytes 6148
  310.3 74.2 %all-to-all-start.1 = ((bf16[32,24,2048]{2,1,0:T(8,128)(2,1)}), bf16[32,24,2048]{2,1,0:T(8,128)(2,1)}, u32[]{:S(2)}, u32[]{:S(2)}) async-start(bf16[32,24,2048]{2,1,0:T(8,128)(2,1)} %bitcast.34), calls=%async_computation.2 | async-start | bytes 6291456 | tf_op jit(solution)/shard_map/all_to_all | solution.py:67
  384.5 8.6 %copy-start.3 = (bf16[64,2048]{1,0:T(8,128)(2,1)S(1)}, bf16[64,2048]{1,0:T(8,128)(2,1)}, u32[]{:S(2)}) copy-start(bf16[64,2048]{1,0:T(8,128)(2,1)} %reduce-scatter.2.cloned.1.call-done) | copy-start | bytes 786436
  384.5 15.3 %copy-start.1 = (bf16[1,128,2048]{2,1,0:T(8,128)(2,1)S(1)}, bf16[1,128,2048]{2,1,0:T(8,128)(2,1)}, u32[]{:S(2)}) copy-start(bf16[1,128,2048]{2,1,0:T(8,128)(2,1)} %param.14) | copy-start | bytes 1572868
  393.3 5.8 %collective-permute-start = (bf16[64,2048]{1,0:T(8,128)(2,1)S(1)}, bf16[64,2048]{1,0:T(8,128)(2,1)S(1)}, u32[]{:S(2)}, u32[]{:S(2)}) collective-permute-start(bf16[64,2048]{1,0:T(8,128)(2,1)S(1)} %fusion.33), channel_id=1, source_target_pairs={{0,8},{8,16},{16,24},{24,0},{1,9},{9,17},{17,25},{25,1},{2,10},{10... | collective-permute-start | bytes 786440 | tf_op jit(solution)/shard_map/ppermute | solution.py:18
Sparse Core Ops, SparseCore 0:
  10.4 51.9 all-gather.3
  64.6 71.8 all-gather.5
  142.9 66.4 reduce-scatter.1
where the time goes:
time: 407 us; the launch traced here: 406 us
  waiting for transfers between devices  262 us (64%)
  blocking collectives  72.9 us (18%)
  matrix products  25.9 us (6%)
  local copies, waits for them, and re-layouts  18 us (4%)
  between operations  13.3 us (3%)
  other arithmetic  9.89 us (2%)
  starting transfers between devices  4.71 us (1%)
    all_to_all x1, blocking collectives, per_device(): lax.all_to_all(send_rows, 'expert', split_axis=0, concat_axis=0, tiled=True)  72.9 us
    all_gather x1, waiting for transfers between devices, per_device(): gathered_keyval = lax.all_gather(w_keyval[0], 'expert', axis=0, tiled=True)  71.6 us
    all_to_all x1, waiting for transfers between devices, send_back(): lax.all_to_all(results, 'expert', split_axis=0, concat_axis=0, tiled=True)  69.5 us
    reduce_scatter x1, waiting for transfers between devices, per_device(): lax.psum_scatter(jnp.dot(attended, out_weight, preferred_element_type=jnp...  64.6 us
    all_gather x1, waiting for transfers between devices, per_device(): row_piece = lax.all_gather(normed, 'expert', axis=0, tiled=True)  50 us
    dot_general x1, matrix products, expert_rows(): jnp.einsum('necd,edf->necf', grouped, gate_up, preferred_element_type=jnp...  10.8 us
  transfers between devices with their start and end apart: 5, of which 5 were waited for; matrix products, arithmetic and copies ran while one was open for 2% of the time, Pallas kernels for 0%

commit v1 on v0

--- a/solution.py
+++ b/solution.py
@@ -91,7 +91,14 @@
     normed = rms_scale(x_wide, gains[0]).astype(jnp.bfloat16)
     kv_index = my_index * head_dev // (heads_total // KV)
     query_weight = w_query[0]
-    gathered_keyval = lax.all_gather(w_keyval[0], "expert", axis=0, tiled=True)
+    ring = [w_keyval[0]]
+    for hop in range(7):
+        ring.append(lax.ppermute(ring[-1], "expert", [(dev, (dev + 1) % 8) for dev in range(8)]))
+    gathered_keyval = jnp.roll(
+        jnp.concatenate(ring[::-1], axis=0),
+        (lax.axis_index("expert") + 1) * ring[0].shape[0],
+        axis=0,
+    )
     head_keyval = lax.dynamic_index_in_dim(gathered_keyval, kv_index, 1, keepdims=False)
     row_piece = lax.all_gather(normed, "expert", axis=0, tiled=True)
     piece_rows = row_piece.shape[0]

time: 407 us -> 410 us (level)
  waiting for transfers between devices: 262 us -> 243 us
  local copies, waits for them, and re-layouts: 18 us -> 36.7 us
    ppermute x0 -> x7, waiting for transfers between devices: none -> 102 us  [per_device(): lax.ppermute(ring[-1], 'expert', [(dev, (dev + 1) % 8) for dev in range(8)])]
    all_gather x1 -> x0, waiting for transfers between devices: 71.6 us -> none  [per_device(): gathered_keyval = lax.all_gather(w_keyval[0], 'expert', axis=0, tiled=True)]
    all_gather x1, waiting for transfers between devices: 50 us -> 0.01 us  [per_device(): row_piece = lax.all_gather(normed, 'expert', axis=0, tiled=True)]
    unnamed x17 -> x34, local copies, waits for them, and re-layouts: 2.74 us -> 20.6 us
  transfers between devices with their start and end apart: 5 -> 11, of which waited for: 5 -> 10; matrix products, arithmetic and copies ran while one was open for 2% -> 6% of each run, Pallas kernels for 0% -> 0%
where the time goes in v1:
time: 410 us; the launch traced here: 409 us
  waiting for transfers between devices  243 us (59%)
  blocking collectives  72.9 us (18%)
  local copies, waits for them, and re-layouts  36.7 us (9%)
  matrix products  26 us (6%)
  between operations  13.6 us (3%)
  other arithmetic  9.88 us (2%)
  starting transfers between devices  7.54 us (2%)
    ppermute x7, waiting for transfers between devices, per_device(): lax.ppermute(ring[-1], 'expert', [(dev, (dev + 1) % 8) for dev in range(8)])  102 us
    all_to_all x1, blocking collectives, per_device(): lax.all_to_all(send_rows, 'expert', split_axis=0, concat_axis=0, tiled=True)  72.9 us
    all_to_all x1, waiting for transfers between devices, send_back(): lax.all_to_all(results, 'expert', split_axis=0, concat_axis=0, tiled=True)  69.5 us
    reduce_scatter x1, waiting for transfers between devices, per_device(): lax.psum_scatter(jnp.dot(attended, out_weight, preferred_element_type=jnp...  65 us
    unnamed x34, local copies, waits for them, and re-layouts  20.6 us
    dot_general x1, matrix products, expert_rows(): jnp.einsum('necd,edf->necf', grouped, gate_up, preferred_element_type=jnp...  10.8 us
  transfers between devices with their start and end apart: 11, of which 10 were waited for; matrix products, arithmetic and copies ran while one was open for 6% of the time, Pallas kernels for 0%

profile of v1, /device:TPU:0, one launch (start us, length us, event | category | flops | bytes accessed | tf_op | source)
XLA Modules:
  0.0 409.4 jit_solution(3040787108882928086)
XLA Ops:
  6.5 1.2 copy.31
  7.7 3.0 collective-permute-start
  10.7 15.0 %collective-permute-done = bf16[256,4,256]{2,0,1:T(8,128)(2,1)S(1)} collective-permute-done((bf16[256,4,256]{2,0,1:T(8,128)(2,1)S(1)}, bf16[256,4,256]{2,0,1:T(8,128)(2,1)S(1)}, u32[]{:S(2)}, u32[]{:S(2)}) %collective-permute-start) | collective-permute-done | bytes 524320 | tf_op jit(solution)/shard_map/ppermute | solution.py:96
  25.7 15.8 %collective-permute-done.1 = bf16[256,4,256]{2,0,1:T(8,128)(2,1)S(1)} collective-permute-done((bf16[256,4,256]{2,0,1:T(8,128)(2,1)S(1)}, bf16[256,4,256]{2,0,1:T(8,128)(2,1)S(1)}, u32[]{:S(2)}, u32[]{:S(2)}) %collective-permute-start.1) | collective-permute-done | bytes 524320 | tf_op jit(solution)/shard_map/ppermute | solution.py:96
  42.6 13.8 %collective-permute-done.2 = bf16[256,4,256]{2,0,1:T(8,128)(2,1)S(1)} collective-permute-done((bf16[256,4,256]{2,0,1:T(8,128)(2,1)S(1)}, bf16[256,4,256]{2,0,1:T(8,128)(2,1)S(1)}, u32[]{:S(2)}, u32[]{:S(2)}) %collective-permute-start.2) | collective-permute-done | bytes 524320 | tf_op jit(solution)/shard_map/ppermute | solution.py:96
  57.2 13.1 %collective-permute-done.3 = bf16[256,4,256]{2,0,1:T(8,128)(2,1)S(1)} collective-permute-done((bf16[256,4,256]{2,0,1:T(8,128)(2,1)S(1)}, bf16[256,4,256]{2,0,1:T(8,128)(2,1)S(1)}, u32[]{:S(2)}, u32[]{:S(2)}) %collective-permute-start.3) | collective-permute-done | bytes 524320 | tf_op jit(solution)/shard_map/ppermute | solution.py:96
  70.4 1.8 fusion.36
  72.2 11.3 %collective-permute-done.4 = bf16[256,4,256]{2,0,1:T(8,128)(2,1)} collective-permute-done((bf16[256,4,256]{2,0,1:T(8,128)(2,1)S(1)}, bf16[256,4,256]{2,0,1:T(8,128)(2,1)}, u32[]{:S(2)}, u32[]{:S(2)}) %collective-permute-start.4) | collective-permute-done | bytes 524320 | tf_op jit(solution)/shard_map/ppermute | solution.py:96
  83.5 20.9 %collective-permute-done.5 = bf16[256,4,256]{2,0,1:T(8,128)(2,1)} collective-permute-done((bf16[256,4,256]{2,0,1:T(8,128)(2,1)}, bf16[256,4,256]{2,0,1:T(8,128)(2,1)}, u32[]{:S(2)}, u32[]{:S(2)}) %collective-permute-start.5) | collective-permute-done | bytes 524320 | tf_op jit(solution)/shard_map/ppermute | solution.py:96
  104.4 12.5 %collective-permute-done.6 = bf16[256,4,256]{2,0,1:T(8,128)(2,1)} collective-permute-done((bf16[256,4,256]{2,0,1:T(8,128)(2,1)}, bf16[256,4,256]{2,0,1:T(8,128)(2,1)}, u32[]{:S(2)}, u32[]{:S(2)}) %collective-permute-start.6) | collective-permute-done | bytes 524320 | tf_op jit(solution)/shard_map/ppermute | solution.py:96
  116.9 1.8 constant_dynamic-update-slice_fusion.15
  118.8 1.9 constant_dynamic-update-slice_fusion.14
  120.6 1.9 constant_dynamic-update-slice_fusion.13
  126.6 1.9 constant_dynamic-update-slice_fusion.7
  128.5 1.9 constant_dynamic-update-slice_fusion.6
  130.4 1.9 constant_dynamic-update-slice_fusion.5
  136.4 2.6 fusion.24
  139.1 2.5 convolution_bitcast_fusion
  142.8 2.4 convolution_convert_fusion
  145.5 1.2 reduce-window.6
  147.2 65.0 %reduce-scatter.2.cloned.1.call-done = bf16[64,2048]{1,0:T(8,128)(2,1)} async-done(((bf16[512,2048]{1,0:T(8,128)(2,1)}), bf16[64,2048]{1,0:T(8,128)(2,1)}) %reduce-scatter.2.cloned.1.call-update) | async-done | bytes 262160 | tf_op jit(solution)/shard_map/reduce_scatter | solution.py:147
  213.4 1.8 fusion.32
  215.2 5.0 %scatter_custom_fusion = bf16[768,2048]{1,0:T(8,128)(2,1)S(1)} fusion(s32[512]{0:T(512)S(1)} %bitcast.123, bf16[]{:T(256)} %constant.113.clone.1, bf16[64,2048]{1,0:T(8,128)(2,1)} %fusion.32), kind=kCustom, calls=%fused_computation.15 | custom fusion | bytes 3407874 | tf_op jit(solution)/shard_map/scatter | solution.py:166
  220.2 72.9 %all_to_all.10 = bf16[32,24,2048]{2,1,0:T(8,128)(2,1)S(1)} all-to-all(bf16[32,24,2048]{2,1,0:T(8,128)(2,1)S(1)} %bitcast.117), channel_id=1, replica_groups=mesh['section'=4,'expert'=8] {'expert'}, dimensions={0} | all-to-all | bytes 6291456 | tf_op jit(solution)/shard_map/all_to_all | solution.py:171
  293.1 10.8 %fusion.5 = f32[8,4,24,1536]{3,2,0,1:T(8,128)S(1)} fusion(bf16[1,4,2048,1536]{3,2,1,0:T(8,128)(2,1)} %param.15, bf16[8,4,24,2048]{3,2,1,0:T(8,128)(2,1)S(1)} %bitcast.118), kind=kOutput, calls=%fused_computation.8 | convolution fusion | flops 4831838208 | bytes 33030144 | tf_op jit(solution)/shard_map/necd,edf->necf/dot_general | solution.py:56
  303.9 7.3 %fusion.12 = bf16[8,4,24,2048]{3,2,0,1:T(8,128)(2,1)S(1)} fusion(bf16[1,4,768,2048]{3,2,1,0:T(8,128)(2,1)} %param.16, f32[8,4,24,1536]{3,2,0,1:T(8,128)S(1)} %fusion.5), kind=kOutput, calls=%fused_computation.11 | convolution fusion | flops 2421030912 | bytes 20447232 | tf_op jit(solution)/shard_map/necf,efd->necd/dot_general | solution.py:61
  311.3 1.9 copy.18
  313.2 4.4 %all-to-all-start.1 = ((bf16[32,24,2048]{2,1,0:T(8,128)(2,1)}), bf16[32,24,2048]{2,1,0:T(8,128)(2,1)}, u32[]{:S(2)}, u32[]{:S(2)}) async-start(bf16[32,24,2048]{2,1,0:T(8,128)(2,1)} %bitcast.35), calls=%async_computation.2 | async-start | bytes 6291456 | tf_op jit(solution)/shard_map/all_to_all | solution.py:67
  317.7 69.5 %all-to-all-done.1 = bf16[32,24,2048]{2,1,0:T(8,128)(2,1)} async-done(((bf16[32,24,2048]{2,1,0:T(8,128)(2,1)}), bf16[32,24,2048]{2,1,0:T(8,128)(2,1)}, u32[]{:S(2)}, u32[]{:S(2)}) %all-to-all-start.1) | async-done | bytes 3145760 | tf_op jit(solution)/shard_map/all_to_all | solution.py:67
  387.3 6.8 %gather_fusion = bf16[512,2048]{1,0:T(8,128)(2,1)S(1)} fusion(bf16[768,2048]{1,0:T(8,128)(2,1)} %bitcast.36, s32[1024]{0:T(1024)S(1)} %pad_clamp_fusion), kind=kCustom, calls=%fused_computation | custom fusion | bytes 4196352 | tf_op jit(solution)/shard_map/gather | solution.py:177
  394.0 1.8 fusion.4
  396.1 5.8 %collective-permute-done.7 = bf16[64,2048]{1,0:T(8,128)(2,1)S(1)} collective-permute-done((bf16[64,2048]{1,0:T(8,128)(2,1)S(1)}, bf16[64,2048]{1,0:T(8,128)(2,1)S(1)}, u32[]{:S(2)}, u32[]{:S(2)}) %collective-permute-start.7) | collective-permute-done | bytes 262176 | tf_op jit(solution)/shard_map/ppermute | solution.py:18
  (65 shorter events, 14.4 us)
Async XLA Ops:
  6.5 136.3 %copy-start = (bf16[1,128,2048]{2,1,0:T(8,128)(2,1)S(1)}, bf16[1,128,2048]{2,1,0:T(8,128)(2,1)}, u32[]{:S(2)}) copy-start(bf16[1,128,2048]{2,1,0:T(8,128)(2,1)} %param.14) | copy-start | bytes 1572868
  6.5 119.2 %copy-start.3 = (bf16[1,256,4,256]{3,2,1,0:T(4,128)(2,1)S(1)}, bf16[1,256,4,256]{3,2,1,0:T(4,128)(2,1)}, u32[]{:S(2)}) copy-start(bf16[1,256,4,256]{3,2,1,0:T(4,128)(2,1)} %param.13) | copy-start | bytes 1572868
  6.5 129.8 %all-gather.2.cloned.1.call-start = ((), (), s32[]{:S(2)}) async-start(), calls=%async_computation.3 | async-start | bytes 2359296 | tf_op jit(solution)/shard_map/all_gather | solution.py:103
  7.7 18.0 %collective-permute-start = (bf16[256,4,256]{2,0,1:T(8,128)(2,1)S(1)}, bf16[256,4,256]{2,0,1:T(8,128)(2,1)S(1)}, u32[]{:S(2)}, u32[]{:S(2)}) collective-permute-start(bf16[256,4,256]{2,0,1:T(8,128)(2,1)S(1)} %bitcast.119), channel_id=1, source_target_pairs={{0,1},{1,2},{2,3},{3,4},{4,5},{5,6},{6,7},{7,0},{8,9},{9,10},{10,1... | collective-permute-start | bytes 1572872 | tf_op jit(solution)/shard_map/ppermute | solution.py:96
  25.7 15.8 %collective-permute-start.1 = (bf16[256,4,256]{2,0,1:T(8,128)(2,1)S(1)}, bf16[256,4,256]{2,0,1:T(8,128)(2,1)S(1)}, u32[]{:S(2)}, u32[]{:S(2)}) collective-permute-start(bf16[256,4,256]{2,0,1:T(8,128)(2,1)S(1)} %collective-permute-done), channel_id=1, source_target_pairs={{0,1},{1,2},{2,3},{3,4},{4,5},{5,6},{6,7},{7,0},{8,9},{9,10},{10,1... | collective-permute-start | bytes 1572872 | tf_op jit(solution)/shard_map/ppermute | solution.py:96
  41.5 14.9 %collective-permute-start.2 = (bf16[256,4,256]{2,0,1:T(8,128)(2,1)S(1)}, bf16[256,4,256]{2,0,1:T(8,128)(2,1)S(1)}, u32[]{:S(2)}, u32[]{:S(2)}) collective-permute-start(bf16[256,4,256]{2,0,1:T(8,128)(2,1)S(1)} %collective-permute-done.1), channel_id=1, source_target_pairs={{0,1},{1,2},{2,3},{3,4},{4,5},{5,6},{6,7},{7,0},{8,9},{9,10},{10,1... | collective-permute-start | bytes 1572872 | tf_op jit(solution)/shard_map/ppermute | solution.py:96
  56.4 14.0 %collective-permute-start.3 = (bf16[256,4,256]{2,0,1:T(8,128)(2,1)S(1)}, bf16[256,4,256]{2,0,1:T(8,128)(2,1)S(1)}, u32[]{:S(2)}, u32[]{:S(2)}) collective-permute-start(bf16[256,4,256]{2,0,1:T(8,128)(2,1)S(1)} %collective-permute-done.2), channel_id=1, source_target_pairs={{0,1},{1,2},{2,3},{3,4},{4,5},{5,6},{6,7},{7,0},{8,9},{9,10},{10,1... | collective-permute-start | bytes 1572872 | tf_op jit(solution)/shard_map/ppermute | solution.py:96
  70.4 13.1 %collective-permute-start.4 = (bf16[256,4,256]{2,0,1:T(8,128)(2,1)S(1)}, bf16[256,4,256]{2,0,1:T(8,128)(2,1)}, u32[]{:S(2)}, u32[]{:S(2)}) collective-permute-start(bf16[256,4,256]{2,0,1:T(8,128)(2,1)S(1)} %collective-permute-done.3), channel_id=1, source_target_pairs={{0,1},{1,2},{2,3},{3,4},{4,5},{5,6},{6,7},{7,0},{8,9},{9,10},{10,1... | collective-permute-start | bytes 1572872 | tf_op jit(solution)/shard_map/ppermute | solution.py:96
  72.2 140.1 %reduce-scatter.2.cloned.1.call-start = ((), (), s32[]{:S(2)}) async-start(), calls=%async_computation.4 | async-start | bytes 2359296 | tf_op jit(solution)/shard_map/reduce_scatter | solution.py:147
  83.5 20.9 %collective-permute-start.5 = (bf16[256,4,256]{2,0,1:T(8,128)(2,1)}, bf16[256,4,256]{2,0,1:T(8,128)(2,1)}, u32[]{:S(2)}, u32[]{:S(2)}) collective-permute-start(bf16[256,4,256]{2,0,1:T(8,128)(2,1)} %collective-permute-done.4), channel_id=1, source_target_pairs={{0,1},{1,2},{2,3},{3,4},{4,5},{5,6},{6,7},{7,0},{8,9},{9,10},{10,1... | collective-permute-start | bytes 1572872 | tf_op jit(solution)/shard_map/ppermute | solution.py:96
  104.4 12.6 %collective-permute-start.6 = (bf16[256,4,256]{2,0,1:T(8,128)(2,1)}, bf16[256,4,256]{2,0,1:T(8,128)(2,1)}, u32[]{:S(2)}, u32[]{:S(2)}) collective-permute-start(bf16[256,4,256]{2,0,1:T(8,128)(2,1)} %collective-permute-done.5), channel_id=1, source_target_pairs={{0,1},{1,2},{2,3},{3,4},{4,5},{5,6},{6,7},{7,0},{8,9},{9,10},{10,1... | collective-permute-start | bytes 1572872 | tf_op jit(solution)/shard_map/ppermute | solution.py:96
  128.5 13.7 %copy-start.7 = (s32[1,512]{1,0:T(1,128)S(1)}, s32[1,512]{1,0:T(1,128)}, u32[]{:S(2)}) copy-start(s32[1,512]{1,0:T(1,128)} %param.19) | copy-start | bytes 6148
  139.0 6.2 %copy-start.5 = (s32[1,64,8]{1,2,0:T(8,128)S(1)}, s32[1,64,8]{1,2,0:T(8,128)}, u32[]{:S(2)}) copy-start(s32[1,64,8]{1,2,0:T(8,128)} %param.17) | copy-start | bytes 6148
  139.0 73.2 %copy-start.2 = (bf16[1,64,2048]{2,1,0:T(8,128)(2,1)S(1)}, bf16[1,64,2048]{2,1,0:T(8,128)(2,1)}, u32[]{:S(2)}) copy-start(bf16[1,64,2048]{2,1,0:T(8,128)(2,1)} %param.10) | copy-start | bytes 786436
  311.2 6.4 %copy-start.6 = (f32[1,64,8]{1,2,0:T(8,128)S(1)}, f32[1,64,8]{1,2,0:T(8,128)}, u32[]{:S(2)}) copy-start(f32[1,64,8]{1,2,0:T(8,128)} %param.18) | copy-start | bytes 6148
  313.2 74.1 %all-to-all-start.1 = ((bf16[32,24,2048]{2,1,0:T(8,128)(2,1)}), bf16[32,24,2048]{2,1,0:T(8,128)(2,1)}, u32[]{:S(2)}, u32[]{:S(2)}) async-start(bf16[32,24,2048]{2,1,0:T(8,128)(2,1)} %bitcast.35), calls=%async_computation.2 | async-start | bytes 6291456 | tf_op jit(solution)/shard_map/all_to_all | solution.py:67
  387.3 15.3 %copy-start.1 = (bf16[1,128,2048]{2,1,0:T(8,128)(2,1)S(1)}, bf16[1,128,2048]{2,1,0:T(8,128)(2,1)}, u32[]{:S(2)}) copy-start(bf16[1,128,2048]{2,1,0:T(8,128)(2,1)} %param.14) | copy-start | bytes 1572868
  387.3 8.6 %copy-start.4 = (bf16[64,2048]{1,0:T(8,128)(2,1)S(1)}, bf16[64,2048]{1,0:T(8,128)(2,1)}, u32[]{:S(2)}) copy-start(bf16[64,2048]{1,0:T(8,128)(2,1)} %reduce-scatter.2.cloned.1.call-done) | copy-start | bytes 786436
  396.0 5.8 %collective-permute-start.7 = (bf16[64,2048]{1,0:T(8,128)(2,1)S(1)}, bf16[64,2048]{1,0:T(8,128)(2,1)S(1)}, u32[]{:S(2)}, u32[]{:S(2)}) collective-permute-start(bf16[64,2048]{1,0:T(8,128)(2,1)S(1)} %fusion.33), channel_id=1, source_target_pairs={{0,8},{8,16},{16,24},{24,0},{1,9},{9,17},{17,25},{25,1},{2,10},{10... | collective-permute-start | bytes 786440 | tf_op jit(solution)/shard_map/ppermute | solution.py:18
Sparse Core Ops, SparseCore 0:
  72.3 62.1 all-gather.1
  145.3 66.9 reduce-scatter.1
